TPU v7x, 32 devices: a whole 2x2x4 slice. The times are simulated.
32 devices in a mesh: ctx: 8 (over z, core), chan: 4 (over y, x).
Axes of the slice: x: 2, y: 2, z: 4, core: 2. Of those that a mesh axis runs over, the one named last changes fastest.
Arguments:
- frames: bfloat16 [2, 9216, 1536], P(None, 'ctx'), may hold values from -6 to 6
- ln_gain: float32 [1536], replicated, may hold values from 0.5 to 1.5
- ln_bias: float32 [1536], replicated, may hold values from -3 to 3
- w_in: bfloat16 [1536, 2, 1536], P('ctx', None, 'chan'), may hold values from -0.15625 to 0.15625
- w_depth: float32 [31, 1536], P(None, 'chan'), may hold values from -1 to 1
- bn_gain: float32 [1536], P('chan'), may hold values from 0.1 to 1.9
- bn_bias: float32 [1536], P('chan'), may hold values from -3 to 3
- w_out: bfloat16 [1536, 1536], P('ctx', 'chan'), may hold values from -0.15625 to 0.15625
- lengths: int32 [2], replicated, may hold values from 2304 to 9216, as said below
- grad_out: bfloat16 [2, 9216, 1536], P(None, 'ctx'), may hold values from -6 to 6
Outputs:
- block_out: bfloat16 [2, 9216, 1536], P(None, 'ctx', 'chan')
- grad_frames: bfloat16 [2, 9216, 1536], P(None, 'ctx', 'chan')
- grad_w_in: float32 [1536, 2, 1536], P('ctx', None, 'chan')
- grad_w_out: float32 [1536, 1536], P('ctx', 'chan')
- grad_w_depth: float32 [31, 1536], P(None, 'chan')
- grad_bn: float32 [2, 1536], P(None, 'chan')
- grad_ln: float32 [2, 1536], P(None, 'chan')
Inputs may be any that keep to these rules, and one draw needn't show every extreme that they name: `lengths`: recording 0 always has all 9216 frames valid.
All inputs are finite; a program needn't handle non-finite values.
Results may differ from a plain program's by a relative error of at most 0.018.
Values may be sent and summed in bfloat16 or wider, within the bound.
A program may use at most 192 MiB of HBM per device.

v0:
```python
import jax
import jax.numpy as jnp
from jax import lax
from jax.sharding import PartitionSpec as P

epsilon = 1e-05


def padded_2(shard, sides, width):
    for axis, dim in sides:
        devices, length = (lax.axis_size(axis), shard.shape[dim])
        up = [(i, (i + 1) % devices) for i in range(devices - 1)]
        down = [(j, i) for i, j in up]
        last = lax.slice_in_dim(shard, length - width, length, axis=dim)
        initial = lax.slice_in_dim(shard, 0, width, axis=dim)
        before = lax.ppermute(last, axis, up)
        after = lax.ppermute(initial, axis, down)
        shard = jnp.concatenate([before, shard, after], axis=dim)
    return shard


def contract(left_op, right_op, left_dim, right_dim):
    return lax.dot_general(
        left_op,
        right_op,
        (((left_dim,), (right_dim,)), ((), ())),
        preferred_element_type=jnp.float32,
    )


def on_device(frames, ln_gain, ln_bias, w_in, w_depth, bn_gain, bn_bias, w_out, lengths, grad_out):
    records, local_len, model_width = frames.shape
    shard_in = w_in.shape[0]
    channels = w_in.shape[2]
    tap_count = w_depth.shape[0]
    margin = (tap_count - 1) // 2
    local_rows = records * local_len
    chan_start = lax.axis_index("chan") * channels
    position = lax.axis_index("ctx") * local_len + jnp.arange(local_len, dtype=jnp.int32)
    valid_mask = (position[None, :] < lengths[:, None]).astype(jnp.float32)[:, :, None]
    frame_count = jnp.sum(lengths.astype(jnp.float32))
    inputs = frames.astype(jnp.float32)
    centred = inputs - jnp.mean(inputs, axis=-1, keepdims=True)
    ln_rstd = lax.rsqrt(jnp.mean(centred * centred, axis=-1, keepdims=True) + epsilon)
    ln_hat = centred * ln_rstd
    normed = (ln_hat * ln_gain + ln_bias).astype(jnp.bfloat16)
    normed_rows = normed.reshape(local_rows, model_width)
    shard_piece = lax.all_gather(w_in, "ctx", axis=0, tiled=True)
    piece_rows = shard_piece.shape[0]
    projected = jnp.dot(
        normed_rows,
        shard_piece.reshape(piece_rows, 2 * channels),
        preferred_element_type=jnp.float32,
    )
    projected = projected.reshape(records, local_len, 2, channels)
    values = projected[:, :, 0]
    gate_vals = jax.nn.sigmoid(projected[:, :, 1])
    glu_out = (values * gate_vals * valid_mask).astype(jnp.bfloat16)
    padded = padded_2(glu_out, (("ctx", 1),), margin).astype(jnp.float32)
    depth_out = jnp.zeros((records, local_len, channels), jnp.float32)
    for offset in range(tap_count):
        depth_out = depth_out + padded[:, offset : offset + local_len] * w_depth[offset]
    bn_mean = lax.psum(jnp.sum(depth_out * valid_mask, axis=(0, 1)), "ctx") / frame_count
    bn_cent = (depth_out - bn_mean) * valid_mask
    bn_var = lax.psum(jnp.sum(bn_cent * bn_cent, axis=(0, 1)), "ctx") / frame_count
    bn_rstd = lax.rsqrt(bn_var + epsilon)
    bn_hat = (depth_out - bn_mean) * bn_rstd
    bn_out = bn_hat * bn_gain + bn_bias
    swish_gate = jax.nn.sigmoid(bn_out)
    activated = (bn_out * swish_gate * valid_mask).astype(jnp.bfloat16)
    act_rows = activated.reshape(local_rows, channels)
    proj_out = contract(act_rows, lax.all_gather(w_out, "ctx", axis=0, tiled=True), 1, 1)
    own_out = lax.psum_scatter(
        proj_out.astype(jnp.bfloat16), "chan", scatter_dimension=1, tiled=True
    ).astype(jnp.float32)
    input_rows = inputs.reshape(local_rows, model_width)
    own_inputs = lax.dynamic_slice_in_dim(input_rows, chan_start, channels, 1)
    block_out = (own_inputs + own_out).astype(jnp.bfloat16).reshape(records, local_len, channels)
    grad_rows = grad_out.reshape(local_rows, model_width)
    picked = grad_rows
    grad_w_out = lax.psum_scatter(
        contract(picked, act_rows, 0, 0).astype(jnp.bfloat16),
        "ctx",
        scatter_dimension=0,
        tiled=True,
    ).astype(jnp.float32)
    picked = grad_rows
    grad_act = jnp.dot(
        picked, lax.all_gather(w_out, "ctx", axis=0, tiled=True), preferred_element_type=jnp.float32
    )
    grad_act = grad_act.reshape(records, local_len, channels)
    grad_bn_out = grad_act * valid_mask * (swish_gate * (1.0 + bn_out * (1.0 - swish_gate)))
    gain_sum, bias_sum = lax.psum(
        (jnp.sum(grad_bn_out * bn_hat, axis=(0, 1)), jnp.sum(grad_bn_out, axis=(0, 1))), "ctx"
    )
    grad_depth = (
        valid_mask
        * (bn_gain * bn_rstd)
        * (grad_bn_out - (bias_sum + bn_hat * gain_sum) / frame_count)
    )
    grad_padded = padded_2(grad_depth, (("ctx", 1),), margin)
    depth_local = jnp.stack(
        [
            jnp.sum(grad_depth * padded[:, offset : offset + local_len], axis=(0, 1))
            for offset in range(tap_count)
        ]
    )
    grad_glu = jnp.zeros((records, local_len, channels), jnp.float32)
    for offset in range(tap_count):
        begin_at = tap_count - 1 - offset
        grad_glu = grad_glu + grad_padded[:, begin_at : begin_at + local_len] * w_depth[offset]
    grad_glu = grad_glu * valid_mask
    grad_values = grad_glu * gate_vals
    grad_gates = grad_glu * values * gate_vals * (1.0 - gate_vals)
    grad_proj = (
        jnp.stack([grad_values, grad_gates], axis=2)
        .astype(jnp.bfloat16)
        .reshape(local_rows, 2 * channels)
    )
    picked = normed_rows
    grad_w_in = lax.psum_scatter(
        contract(picked, grad_proj, 0, 0)
        .reshape(shard_in * lax.axis_size("ctx"), 2, channels)
        .astype(jnp.bfloat16),
        "ctx",
        scatter_dimension=0,
        tiled=True,
    ).astype(jnp.float32)
    shard_piece = lax.all_gather(w_in, "ctx", axis=0, tiled=True)
    grad_part = contract(grad_proj, shard_piece.reshape(shard_piece.shape[0], 2 * channels), 1, 1)
    hat_rows = ln_hat.reshape(local_rows, model_width)
    rstd_rows = ln_rstd.reshape(local_rows, 1)
    own_hat = lax.dynamic_slice_in_dim(hat_rows, chan_start, channels, 1)
    own_grad = lax.psum_scatter(
        grad_part.astype(jnp.bfloat16), "chan", scatter_dimension=1, tiled=True
    ).astype(jnp.float32)
    own_gain = lax.dynamic_slice_in_dim(ln_gain, chan_start, channels, 0)
    own_scaled = own_grad * own_gain
    first_rows, second_rows = lax.psum(
        (jnp.sum(own_scaled, axis=1), jnp.sum(own_scaled * own_hat, axis=1)), "chan"
    )
    own_dx = rstd_rows * (
        own_scaled
        - first_rows[:, None] / model_width
        - own_hat * (second_rows[:, None] / model_width)
    )
    own_cotangent = lax.dynamic_slice_in_dim(grad_rows, chan_start, channels, 1).astype(jnp.float32)
    grad_frames = (
        (own_dx + own_cotangent).astype(jnp.bfloat16).reshape(records, local_len, channels)
    )
    ln_local = jnp.stack([jnp.sum(own_grad * own_hat, axis=0), jnp.sum(own_grad, axis=0)])
    grad_w_depth, grad_ln = lax.psum((depth_local, ln_local), "ctx")
    grad_bn = jnp.stack([gain_sum, bias_sum])
    return (block_out, grad_frames, grad_w_in, grad_w_out, grad_w_depth, grad_bn, grad_ln)


def solution(mesh):
    in_specs = (
        P(None, "ctx", None),
        P(),
        P(),
        P("ctx", None, "chan"),
        P(None, "chan"),
        P("chan"),
        P("chan"),
        P("ctx", "chan"),
        P(),
        P(None, "ctx", None),
    )
    out_specs = (
        P(None, "ctx", "chan"),
        P(None, "ctx", "chan"),
        P("ctx", None, "chan"),
        P("ctx", "chan"),
        P(None, "chan"),
        P(None, "chan"),
        P(None, "chan"),
    )
    return jax.shard_map(
        on_device, mesh=mesh, in_specs=in_specs, out_specs=out_specs, check_vma=False
    )
```

profile of v0, /device:TPU:0, one launch (start us, length us, event | category | flops | bytes accessed | tf_op | source)
XLA Modules:
  0.0 555.2 jit_solution(12352163008588690644)
XLA Ops:
  8.7 1.9 slice_reduce_fusion.30
  10.6 1.7 slice_reduce_fusion.29
  12.2 4.2 convert_reduce_fusion
  17.3 2.0 multiply_reduce_fusion
  19.4 10.8 %subtract_multiply_fusion = (f32[2,1152,1536]{2,1,0:T(8,128)}, bf16[2,1152,1536]{2,1,0:T(8,128)(2,1)}) fusion(bf16[2,1152,1536]{2,1,0:T(8,128)(2,1)} %param.10, f32[2,1152]{1,0:T(2,128)S(1)} %add_rsqrt_fusion, f32[2,1152]{1,0:T(2,128)S(1)} %broadcast_multiply_fusion.2, f32[1536]{0:T(1024)S(1)} %copy-done.42, f32[1536]{0:T(1024)S(1)} %copy-done.41), kind=kLoop, calls=%fused_computation.30 | loop fusion | flops 21233664 | bytes 28342272 | tf_op jit(solution)/shard_map/mul | solution.py:45
  30.1 13.6 %all-gather.3.cloned.1.call-done = bf16[1536,2,384]{2,1,0:T(2,128)(2,1)} async-done(((bf16[192,2,384]{2,1,0:T(2,128)(2,1)}), bf16[1536,2,384]{2,1,0:T(2,128)(2,1)}) %all-gather.3.cloned.1.call-update) | async-done | bytes 2359312 | tf_op jit(solution)/shard_map/all_gather | solution.py:48
  43.8 2.1 copy.50
  45.9 2.8 copy.31
  48.8 8.7 %fusion = f32[2,1152,2,384]{3,1,2,0:T(8,128)S(1)} fusion(bf16[2,384,1536,1]{2,1,0,3:T(8,128)(2,1)} %bitcast.89, bf16[2,1152,1536]{2,1,0:T(8,128)(2,1)} %get-tuple-element.110), kind=kOutput, calls=%fused_computation.35 | convolution fusion | flops 5435817984 | bytes 16515072 | tf_op jit(solution)/shard_map/dot_general | solution.py:50
  58.7 1.8 copy-done.3
  61.7 2.1 collective-permute-start
  63.8 1.3 collective-permute-start.1
  65.7 1.9 collective-permute-done.1
  67.5 8.8 %concatenate.38 = bf16[2,1182,384]{2,1,0:T(8,128)(2,1)S(1)} concatenate(bf16[2,15,384]{2,1,0:T(8,128)(2,1)S(1)} %collective-permute-done, bf16[2,1152,384]{2,1,0:T(8,128)(2,1)} %copy-done.6, bf16[2,15,384]{2,1,0:T(8,128)(2,1)S(1)} %collective-permute-done.1), dimensions={1} | concatenate | bytes 3631104 | tf_op jit(solution)/shard_map/concatenate | solution.py:18
  77.3 15.3 %multiply_reduce_fusion.34 = (f32[384]{0:T(512)}, f32[2,1152,384]{2,1,0:T(8,128)S(1)}) fusion(f32[2,1152]{1,0:T(2,128)S(1)} %compare_convert_fusion, f32[384]{0:T(512)S(1)} %copy-done.39, f32[2,1182,384]{2,1,0:T(8,128)S(1)} %convert_element_type.79, f32[384]{0:T(512)S(1)} %copy-done.40, f32[384]{0:T(512)S(1)} %copy-done.10, f32[384]{0:T(512)S(1)} %copy-done.11, ...), kind=kLoop, calls=%fused_computation.209 | loop fusion | flops 55737984 | bytes 113304576 | tf_op jit(solution)/shard_map/reduce_sum | solution.py:63
  92.6 16.8 %psum.56 = f32[384]{0:T(512)} all-reduce(f32[384]{0:T(512)} %get-tuple-element.107), channel_id=1, replica_groups=mesh['ctx'=8,'chan'=4] {'ctx'}, use_global_device_ids=true, to_apply=%region_3.0 | all-reduce | flops 384 | bytes 3072 | tf_op jit(solution)/shard_map/psum | solution.py:63
  109.4 1.3 broadcast_divide_fusion
  112.4 14.7 %psum.57 = f32[384]{0:T(512)} all-reduce(f32[384]{0:T(512)} %multiply_reduce_fusion.33), channel_id=1, replica_groups=mesh['ctx'=8,'chan'=4] {'ctx'}, use_global_device_ids=true, to_apply=%region_6.0 | all-reduce | flops 384 | bytes 3072 | tf_op jit(solution)/shard_map/psum | solution.py:65
  127.2 1.9 fusion.110
  129.1 10.3 %fusion.108 = (f32[384]{0:T(512)}, f32[384]{0:T(512)}, bf16[2,1152,384]{2,1,0:T(8,128)(2,1)}, f32[2,1152,384]{2,1,0:T(8,128)}) fusion(f32[384]{0:T(512)} %get-tuple-element.106, f32[2,1152,384]{2,1,0:T(8,128)S(1)} %get-tuple-element.108, f32[384]{0:T(512)} %copy-done.28, f32[2,1152]{1,0:T(2,128)S(1)} %compare_convert_fusion, f32[384]{0:T(512)} %param.16, ...), kind=kOutput, calls=%fused_computation.260 | convolution fusion | flops 2734717952 | bytes 17123328 | tf_op jit(solution)/shard_map/dot_general | solution.py:88
  139.4 14.3 %all-reduce.1 = (f32[384]{0:T(512)}, f32[384]{0:T(512)}) all-reduce(f32[384]{0:T(512)} %get-tuple-element.62, f32[384]{0:T(512)} %get-tuple-element.61), channel_id=1, replica_groups=mesh['ctx'=8,'chan'=4] {'ctx'}, use_global_device_ids=true, to_apply=%region_11.0 | all-reduce | flops 768 | bytes 6144 | tf_op jit(solution)/shard_map/psum | solution.py:93
  153.7 40.0 %multiply_reduce_fusion.1 = (f32[384]{0:T(512)}, f32[384]{0:T(512)}, f32[384]{0:T(512)}, f32[384]{0:T(512)}, f32[384]{0:T(512)}, /*index=5*/f32[384]{0:T(512)}, ...) fusion(f32[2,1182,384]{2,1,0:T(8,128)} %copy-done, ...), kind=kLoop, calls=%fused_computation.169 | loop fusion | flops 38921472 | bytes 74362368 | tf_op jit(solution)/shard_map/reduce_sum | solution.py:104
  194.3 1.3 collective-permute-start.2
  195.6 3.7 collective-permute-start.3
  199.3 7.0 %fusion.106 = bf16[1536,384]{0,1:T(8,128)(2,1)} fusion(bf16[2,1152,384]{2,1,0:T(8,128)(2,1)S(1)} %copy-done.64, bf16[2,1152,1536]{2,1,0:T(8,128)(2,1)} %param.19), kind=kOutput, calls=%fused_computation.216 | convolution fusion | flops 2718498816 | bytes 10027008 | tf_op jit(solution)/shard_map/dot_general | solution.py:23
  206.3 2.4 copy.47
  208.9 33.2 %multiply_bitcast_fusion.1 = (bf16[2,1152,1,384]{3,1,0,2:T(8,128)(2,1)S(1)}, f32[2,1152,384]{2,1,0:T(8,128)S(1)}) fusion(f32[2,1152,2,384]{3,1,2,0:T(8,128)} %copy-done.3, f32[2,1152]{1,0:T(2,128)S(1)} %compare_convert_fusion, f32[384]{0:T(512)} %get-tuple-element.94, f32[2,1152,384]{2,1,0:T(8,128)S(1)} %get-tuple-element.102, ...), kind=kLoop, calls=%fused_computation.201 | loop fusion | flops 85819392 | bytes 12535296 | tf_op jit(solution)/shard_map/stack | solution.py:116
  242.2 4.2 multiply_bitcast_fusion
  246.8 34.2 %copy.33 = bf16[2,1152,2,384]{3,2,1,0:T(2,128)(2,1)S(1)} copy(bf16[2,1152,2,384]{3,1,0,2:T(8,128)(2,1)S(1)} %maximum_convert_fusion) | data formatting | bytes 7077888 | tf_op jit(solution)/shard_map/convert_element_type | solution.py:117
  281.0 2.4 copy.51
  283.4 5.8 %copy.34 = bf16[768,2304]{1,0:T(8,128)(2,1)} copy(bf16[768,2304]{0,1:T(8,128)(2,1)} %bitcast.81) | data formatting | bytes 7077888 | tf_op jit(solution)/shard_map/dot_general | solution.py:23
  289.3 10.0 %convolution_convert_fusion.2 = bf16[1536,2,384]{2,0,1:T(8,128)(2,1)} fusion(bf16[2304,1536,1]{1,0,2:T(8,128)(2,1)} %bitcast.86, bf16[2,384,2304]{2,1,0:T(8,128)(2,1)} %bitcast.87), kind=kOutput, calls=%fused_computation.212 | convolution fusion | flops 5436997632 | bytes 12976128 | tf_op jit(solution)/shard_map/dot_general | solution.py:23
  299.4 8.5 %convolution_convert_fusion.1 = bf16[2304,1536]{1,0:T(8,128)(2,1)} fusion(bf16[2304,384]{1,0:T(8,128)(2,1)} %bitcast.95, bf16[1536,384]{1,0:T(8,128)(2,1)} %all-gather.5.cloned.1.call-done), kind=kOutput, calls=%fused_computation.32 | convolution fusion | flops 2721447936 | bytes 10027008 | tf_op jit(solution)/shard_map/dot_general | solution.py:23
  307.9 10.2 %copy.43 = bf16[2304,1536]{0,1:T(8,128)(2,1)} copy(bf16[2304,1536]{1,0:T(8,128)(2,1)} %convolution_convert_fusion.1) | data formatting | bytes 14155776
  318.3 10.3 %convolution_convert_fusion = bf16[2304,1536]{1,0:T(8,128)(2,1)} fusion(bf16[2304,768]{1,0:T(8,128)(2,1)} %bitcast.82, bf16[1536,768]{1,0:T(8,128)(2,1)} %bitcast.85), kind=kOutput, calls=%fused_computation.31 | convolution fusion | flops 5439356928 | bytes 12976128 | tf_op jit(solution)/shard_map/dot_general | solution.py:23
  328.6 9.9 %copy.45 = bf16[2304,1536]{0,1:T(8,128)(2,1)} copy(bf16[2304,1536]{1,0:T(8,128)(2,1)} %convolution_convert_fusion) | data formatting | bytes 14155776
  340.6 10.9 %bitcast_convert_fusion = f32[2304,1536]{1,0:T(8,128)} fusion(bf16[2,1152,1536]{2,1,0:T(8,128)(2,1)} %param.10), kind=kLoop, calls=%fused_computation.264 | loop fusion | flops 3538944 | bytes 21233664 | tf_op jit(solution)/shard_map/reshape | solution.py:76
  351.7 6.0 %multiply_reduce_fusion.2 = (f32[384]{0:T(512)S(1)}, f32[384]{0:T(512)S(1)}, f32[384]{0:T(512)S(1)}, f32[384]{0:T(512)S(1)}, f32[384]{0:T(512)S(1)}, /*index=5*/...) fusion(f32[2,1152,384]{2,1,0:T(8,128)S(1)} %get-tuple-element.1, ...), kind=kLoop, calls=%fused_computation.170 | loop fusion | flops 22998144 | bytes 49565184 | tf_op jit(solution)/shard_map/reduce_sum | solution.py:104
  360.8 2.1 copy.37
  363.0 50.2 %reduce-scatter.13.cloned.1.call-done = bf16[384,2304]{1,0:T(8,128)(2,1)} async-done(((bf16[1536,2304]{1,0:T(8,128)(2,1)}), bf16[384,2304]{1,0:T(8,128)(2,1)}) %reduce-scatter.13.cloned.1.call-update) | async-done | bytes 1769488
  413.2 2.8 copy.44
  415.9 3.6 add_convert_fusion.1
  419.5 73.1 %reduce-scatter.15.cloned.1.call-done = bf16[384,2304]{1,0:T(8,128)(2,1)} async-done(((bf16[1536,2304]{1,0:T(8,128)(2,1)}), bf16[384,2304]{1,0:T(8,128)(2,1)}) %reduce-scatter.15.cloned.1.call-update) | async-done | bytes 1769488
  492.7 2.8 copy.46
  495.4 3.2 fusion.11
  498.7 29.4 %all-reduce = (f32[31,384]{1,0:T(8,128)}, f32[2,384]{1,0:T(2,128)}) all-reduce(f32[31,384]{1,0:T(8,128)S(1)} %stack.157, f32[2,384]{1,0:T(2,128)S(1)} %pad_maximum_fusion.3), channel_id=1, replica_groups=mesh['ctx'=8,'chan'=4] {'ctx'}, use_global_device_ids=true, to_apply=%region_50.0 | all-reduce | flops 12672 | bytes 101376 | tf_op jit(solution)/shard_map/psum | solution.py:152
  528.2 15.4 %all-reduce.2 = (f32[2304]{0:T(1024)S(1)}, f32[2304]{0:T(1024)S(1)}) all-reduce(f32[2304]{0:T(1024)S(1)} %get-tuple-element.29, f32[2304]{0:T(1024)S(1)} %get-tuple-element.63), channel_id=1, replica_groups=mesh['ctx'=8,'chan'=4] {'chan'}, use_global_device_ids=true, to_apply=%region_16.0 | all-reduce | flops 4608 | bytes 36864 | tf_op jit(solution)/shard_map/psum | solution.py:139
  543.6 4.5 fusion.9
  (201 shorter events, 14.3 us)
Async XLA Ops:
  7.2 36.6 %all-gather.3.cloned.1.call-start = ((), (), s32[]{:S(2)}) async-start(), calls=%async_computation.4 | async-start | bytes 2654208 | tf_op jit(solution)/shard_map/all_gather | solution.py:48
  7.9 121.2 %all-gather.5.cloned.1.call-start = ((), (), s32[]{:S(2)}) async-start(), calls=%async_computation.5 | async-start | bytes 1327104 | tf_op jit(solution)/shard_map/all_gather | solution.py:72
  8.6 350.3 %reduce-scatter.17.cloned.1.call-start = ((), (), s32[]{:S(2)}) async-start(), calls=%async_computation.9 | async-start | bytes 1327104
  12.2 5.0 copy-start.2
  17.2 2.0 copy-start.63
  17.3 2.1 copy-start.41
  17.3 2.1 copy-start.42
  19.3 10.9 %copy-start.7 = (f32[2,1152]{1,0:T(2,128)}, f32[2,1152]{1,0:T(2,128)S(1)}, u32[]{:S(2)}) copy-start(f32[2,1152]{1,0:T(2,128)S(1)} %add_rsqrt_fusion) | copy-start | bytes 27652
  45.9 11.6 %copy-start.5 = (bf16[192,8,2,384]{3,1,2,0:T(8,128)(2,1)}, bf16[192,8,2,384]{3,1,2,0:T(8,128)(2,1)S(1)}, u32[]{:S(2)}) copy-start(bf16[192,8,2,384]{3,1,2,0:T(8,128)(2,1)S(1)} %copy.50) | copy-start | bytes 7077892
  57.5 2.9 copy-start.3
  60.4 1.2 copy-start.6
  61.7 4.0 collective-permute-start
  63.8 3.8 collective-permute-start.1
  76.5 0.7 copy-start.29
  76.5 0.7 copy-start.30
  76.6 0.7 copy-start.35
  76.6 0.7 copy-start.40
  76.9 15.7 %copy-start = (f32[2,1182,384]{2,1,0:T(8,128)}, f32[2,1182,384]{2,1,0:T(8,128)S(1)}, u32[]{:S(2)}) copy-start(f32[2,1182,384]{2,1,0:T(8,128)S(1)} %convert_element_type.79) | copy-start | bytes 10893316
  92.6 46.8 %copy-start.4 = (f32[2,1152,384]{2,1,0:T(8,128)}, f32[2,1152,384]{2,1,0:T(8,128)S(1)}, u32[]{:S(2)}) copy-start(f32[2,1152,384]{2,1,0:T(8,128)S(1)} %get-tuple-element.108) | copy-start | bytes 10616836
  153.7 45.6 %copy-start.64 = (bf16[2,1152,384]{2,1,0:T(8,128)(2,1)S(1)}, bf16[2,1152,384]{2,1,0:T(8,128)(2,1)}, u32[]{:S(2)}) copy-start(bf16[2,1152,384]{2,1,0:T(8,128)(2,1)} %get-tuple-element.111) | copy-start | bytes 5308420
  194.3 14.6 %collective-permute-start.2 = (f32[2,15,384]{2,1,0:T(8,128)}, f32[2,15,384]{2,1,0:T(8,128)}, u32[]{:S(2)}, u32[]{:S(2)}) collective-permute-start(f32[2,15,384]{2,1,0:T(8,128)} %get-tuple-element.112), channel_id=1, source_target_pairs={{4,0},{8,4},{12,8},{16,12},{20,16},{24,20},{28,24},{5,1},{9,5},{13... | collective-permute-start | bytes 138248 | tf_op jit(solution)/shard_map/ppermute | solution.py:17
  195.6 13.3 %collective-permute-start.3 = (f32[2,15,384]{2,1,0:T(8,128)}, f32[2,15,384]{2,1,0:T(8,128)}, u32[]{:S(2)}, u32[]{:S(2)}) collective-permute-start(f32[2,15,384]{2,1,0:T(8,128)} %get-tuple-element.113), channel_id=1, source_target_pairs={{0,4},{4,8},{8,12},{12,16},{16,20},{20,24},{24,28},{1,5},{5,9},{9,... | collective-permute-start | bytes 138248 | tf_op jit(solution)/shard_map/ppermute | solution.py:16
  208.7 152.1 %reduce-scatter.11.cloned.1.call-start = ((), (), s32[]{:S(2)}) async-start(), calls=%async_computation.6 | async-start | bytes 2654208 | tf_op jit(solution)/shard_map/reduce_scatter | solution.py:121
  299.3 113.9 %reduce-scatter.13.cloned.1.call-start = ((), (), s32[]{:S(2)}) async-start(), calls=%async_computation.7 | async-start | bytes 8847360
  318.1 174.6 %reduce-scatter.15.cloned.1.call-start = ((), (), s32[]{:S(2)}) async-start(), calls=%async_computation.8 | async-start | bytes 8847360
  338.5 0.7 copy-start.8
  340.6 10.9 %copy-start.62 = (f32[384]{0:T(512)S(1)}, f32[384]{0:T(512)}, u32[]{:S(2)}) copy-start(f32[384]{0:T(512)} %get-tuple-element.98) | copy-start | bytes 4612
  340.6 10.9 %copy-start.61 = (f32[384]{0:T(512)S(1)}, f32[384]{0:T(512)}, u32[]{:S(2)}) copy-start(f32[384]{0:T(512)} %get-tuple-element.99) | copy-start | bytes 4612
  340.6 10.9 %copy-start.1 = (f32[2,1182,384]{2,1,0:T(8,128)S(1)}, f32[2,1182,384]{2,1,0:T(8,128)}, u32[]{:S(2)}) copy-start(f32[2,1182,384]{2,1,0:T(8,128)} %copy-done) | copy-start | bytes 10893316
  351.5 6.3 %copy-start.60 = (f32[384]{0:T(512)S(1)}, f32[384]{0:T(512)}, u32[]{:S(2)}) copy-start(f32[384]{0:T(512)} %get-tuple-element.47) | copy-start | bytes 4612
  351.5 6.3 %copy-start.59 = (f32[384]{0:T(512)S(1)}, f32[384]{0:T(512)}, u32[]{:S(2)}) copy-start(f32[384]{0:T(512)} %get-tuple-element.46) | copy-start | bytes 4612
  351.5 6.4 %copy-start.58 = (f32[384]{0:T(512)S(1)}, f32[384]{0:T(512)}, u32[]{:S(2)}) copy-start(f32[384]{0:T(512)} %get-tuple-element.45) | copy-start | bytes 4612
  351.5 6.4 %copy-start.57 = (f32[384]{0:T(512)S(1)}, f32[384]{0:T(512)}, u32[]{:S(2)}) copy-start(f32[384]{0:T(512)} %get-tuple-element.44) | copy-start | bytes 4612
  351.5 6.4 %copy-start.56 = (f32[384]{0:T(512)S(1)}, f32[384]{0:T(512)}, u32[]{:S(2)}) copy-start(f32[384]{0:T(512)} %get-tuple-element.43) | copy-start | bytes 4612
  351.6 6.4 %copy-start.55 = (f32[384]{0:T(512)S(1)}, f32[384]{0:T(512)}, u32[]{:S(2)}) copy-start(f32[384]{0:T(512)} %get-tuple-element.42) | copy-start | bytes 4612
  351.6 6.4 %copy-start.54 = (f32[384]{0:T(512)S(1)}, f32[384]{0:T(512)}, u32[]{:S(2)}) copy-start(f32[384]{0:T(512)} %get-tuple-element.41) | copy-start | bytes 4612
  351.6 6.4 %copy-start.53 = (f32[384]{0:T(512)S(1)}, f32[384]{0:T(512)}, u32[]{:S(2)}) copy-start(f32[384]{0:T(512)} %get-tuple-element.40) | copy-start | bytes 4612
  351.6 6.4 %copy-start.52 = (f32[384]{0:T(512)S(1)}, f32[384]{0:T(512)}, u32[]{:S(2)}) copy-start(f32[384]{0:T(512)} %get-tuple-element.39) | copy-start | bytes 4612
  351.6 6.4 %copy-start.51 = (f32[384]{0:T(512)S(1)}, f32[384]{0:T(512)}, u32[]{:S(2)}) copy-start(f32[384]{0:T(512)} %get-tuple-element.38) | copy-start | bytes 4612
  351.6 6.4 %copy-start.50 = (f32[384]{0:T(512)S(1)}, f32[384]{0:T(512)}, u32[]{:S(2)}) copy-start(f32[384]{0:T(512)} %get-tuple-element.37) | copy-start | bytes 4612
  351.6 6.5 %copy-start.49 = (f32[384]{0:T(512)S(1)}, f32[384]{0:T(512)}, u32[]{:S(2)}) copy-start(f32[384]{0:T(512)} %get-tuple-element.36) | copy-start | bytes 4612
  351.6 6.5 %copy-start.48 = (f32[384]{0:T(512)S(1)}, f32[384]{0:T(512)}, u32[]{:S(2)}) copy-start(f32[384]{0:T(512)} %get-tuple-element.35) | copy-start | bytes 4612
  351.6 6.5 %copy-start.47 = (f32[384]{0:T(512)S(1)}, f32[384]{0:T(512)}, u32[]{:S(2)}) copy-start(f32[384]{0:T(512)} %get-tuple-element.34) | copy-start | bytes 4612
  351.6 6.5 %copy-start.46 = (f32[384]{0:T(512)S(1)}, f32[384]{0:T(512)}, u32[]{:S(2)}) copy-start(f32[384]{0:T(512)} %get-tuple-element.33) | copy-start | bytes 4612
  351.7 6.5 %copy-start.45 = (f32[384]{0:T(512)S(1)}, f32[384]{0:T(512)}, u32[]{:S(2)}) copy-start(f32[384]{0:T(512)} %get-tuple-element.32) | copy-start | bytes 4612
  351.7 6.5 %copy-start.44 = (f32[384]{0:T(512)S(1)}, f32[384]{0:T(512)}, u32[]{:S(2)}) copy-start(f32[384]{0:T(512)} %get-tuple-element.31) | copy-start | bytes 4612
  351.7 6.5 %copy-start.43 = (f32[384]{0:T(512)S(1)}, f32[384]{0:T(512)}, u32[]{:S(2)}) copy-start(f32[384]{0:T(512)} %get-tuple-element.30) | copy-start | bytes 4612
  495.4 48.2 %copy-start.9 = (f32[2304]{0:T(1024)S(1)}, f32[2304]{0:T(1024)}, u32[]{:S(2)}) copy-start(f32[2304]{0:T(1024)} %rsqrt.20) | copy-start | bytes 27652
  (27 other events, 18.1 us)
Sparse Core Ops, SparseCore 0:
  9.6 34.1 all-gather.2
  45.4 22.0 all-gather.4
  208.8 31.2 reduce-scatter.16
  299.4 35.3 reduce-scatter.10
  337.8 75.3 reduce-scatter.12
  416.1 76.5 reduce-scatter.14
where the time goes:
time: 565 us; the launch traced here: 555 us
  other arithmetic  145 us (26%)
  waiting for transfers between devices  140 us (25%)
  local copies, waits for them, and re-layouts  99.7 us (18%)
  blocking collectives  90.7 us (16%)
  matrix products  54.8 us (10%)
  between operations  15.4 us (3%)
  starting transfers between devices  8.95 us (2%)
    unnamed x9, waiting for transfers between devices  125 us
    reduce_sum x2, other arithmetic, on_device(): jnp.sum(grad_depth * padded[:, offset:offset + local_len], axis=(0, 1))  46 us
    unnamed x140, local copies, waits for them, and re-layouts  42.2 us
    another operation x2, other arithmetic, on_device(): jnp.stack([grad_values, grad_gates], axis=2).astype(jnp.bfloat16)  37.4 us
    dot_general x4, matrix products, contract(): lax.dot_general(left_op, right_op, (((left_dim,), (right_dim,)), ((), ())...  35.8 us
    convert_element_type x1, local copies, waits for them, and re-layouts, on_device(): grad_proj = jnp.stack([grad_values, grad_gates], axis=2).astype(jnp.bfloa...  34.2 us
    psum x1, blocking collectives, on_device(): grad_w_depth, grad_ln = lax.psum((depth_local, ln_local), 'ctx')  29.4 us
    psum x1, blocking collectives, on_device(): lax.psum(jnp.sum(depth_out * valid_mask, axis=(0, 1)), 'ctx') / frame_count  16.8 us
  transfers between devices with their start and end apart: 10, of which 4 were waited for; matrix products, arithmetic and copies ran while one was open for 42% of the time, Pallas kernels for 0%

commit v1 on v0

--- a/solution.py
+++ b/solution.py
@@ -60,7 +60,10 @@
     depth_out = jnp.zeros((records, local_len, channels), jnp.float32)
     for offset in range(tap_count):
         depth_out = depth_out + padded[:, offset : offset + local_len] * w_depth[offset]
-    bn_mean = lax.psum(jnp.sum(depth_out * valid_mask, axis=(0, 1)), "ctx") / frame_count
+    bn_mean = (
+        jnp.sum(lax.all_gather(jnp.sum(depth_out * valid_mask, axis=(0, 1)), "ctx"), axis=0)
+        / frame_count
+    )
     bn_cent = (depth_out - bn_mean) * valid_mask
     bn_var = lax.psum(jnp.sum(bn_cent * bn_cent, axis=(0, 1)), "ctx") / frame_count
     bn_rstd = lax.rsqrt(bn_var + epsilon)

time: 565 us -> 564 us (level)
    psum x1 -> x0, blocking collectives: 16.8 us -> none  [on_device(): lax.psum(jnp.sum(depth_out * valid_mask, axis=(0, 1)), 'ctx') / frame_count]
    all_gather x0 -> x1, blocking collectives: none -> 14.1 us  [on_device(): lax.all_gather(jnp.sum(depth_out * valid_mask, axis=(0, 1)), 'ctx')]
    unnamed x140 -> x141, local copies, waits for them, and re-layouts: 42.2 us -> 42.2 us
where the time goes in v1:
time: 564 us; the launch traced here: 554 us
  other arithmetic  146 us (26%)
  waiting for transfers between devices  140 us (25%)
  local copies, waits for them, and re-layouts  99.7 us (18%)
  blocking collectives  88.7 us (16%)
  matrix products  54.9 us (10%)
  between operations  15.6 us (3%)
  starting transfers between devices  8.95 us (2%)
    unnamed x9, waiting for transfers between devices  125 us
    reduce_sum x2, other arithmetic, on_device(): jnp.sum(grad_depth * padded[:, offset:offset + local_len], axis=(0, 1))  46 us
    unnamed x141, local copies, waits for them, and re-layouts  42.2 us
    another operation x2, other arithmetic, on_device(): jnp.stack([grad_values, grad_gates], axis=2).astype(jnp.bfloat16)  37.4 us
    dot_general x4, matrix products, contract(): lax.dot_general(left_op, right_op, (((left_dim,), (right_dim,)), ((), ())...  35.8 us
    convert_element_type x1, local copies, waits for them, and re-layouts, on_device(): grad_proj = jnp.stack([grad_values, grad_gates], axis=2).astype(jnp.bfloa...  34.2 us
    psum x1, blocking collectives, on_device(): grad_w_depth, grad_ln = lax.psum((depth_local, ln_local), 'ctx')  29.4 us
    psum x1, blocking collectives, on_device(): lax.psum(jnp.sum(bn_cent * bn_cent, axis=(0, 1)), 'ctx') / frame_count  15.5 us
  transfers between devices with their start and end apart: 10, of which 4 were waited for; matrix products, arithmetic and copies ran while one was open for 42% of the time, Pallas kernels for 0%

profile of v1, /device:TPU:0, one launch (start us, length us, event | category | flops | bytes accessed | tf_op | source)
XLA Modules:
  0.0 554.2 jit_solution(5017218447660173859)
XLA Ops:
  8.7 1.9 slice_reduce_fusion.30
  10.6 1.7 slice_reduce_fusion.29
  12.2 4.2 convert_reduce_fusion
  17.3 2.0 multiply_reduce_fusion
  19.4 10.8 %subtract_multiply_fusion = (f32[2,1152,1536]{2,1,0:T(8,128)}, bf16[2,1152,1536]{2,1,0:T(8,128)(2,1)}) fusion(bf16[2,1152,1536]{2,1,0:T(8,128)(2,1)} %param.10, f32[2,1152]{1,0:T(2,128)S(1)} %add_rsqrt_fusion, f32[2,1152]{1,0:T(2,128)S(1)} %broadcast_multiply_fusion.2, f32[1536]{0:T(1024)S(1)} %copy-done.42, f32[1536]{0:T(1024)S(1)} %copy-done.41), kind=kLoop, calls=%fused_computation.30 | loop fusion | flops 21233664 | bytes 28342272 | tf_op jit(solution)/shard_map/mul | solution.py:45
  30.2 13.6 %all-gather.5.cloned.1.call-done = bf16[1536,2,384]{2,1,0:T(2,128)(2,1)} async-done(((bf16[192,2,384]{2,1,0:T(2,128)(2,1)}), bf16[1536,2,384]{2,1,0:T(2,128)(2,1)}) %all-gather.5.cloned.1.call-update) | async-done | bytes 2359312 | tf_op jit(solution)/shard_map/all_gather | solution.py:48
  43.8 2.1 copy.50
  45.9 2.8 copy.31
  48.8 8.7 %fusion = f32[2,1152,2,384]{3,1,2,0:T(8,128)S(1)} fusion(bf16[2,384,1536,1]{2,1,0,3:T(8,128)(2,1)} %bitcast.89, bf16[2,1152,1536]{2,1,0:T(8,128)(2,1)} %get-tuple-element.110), kind=kOutput, calls=%fused_computation.35 | convolution fusion | flops 5435817984 | bytes 16515072 | tf_op jit(solution)/shard_map/dot_general | solution.py:50
  58.7 1.8 copy-done.3
  61.7 2.1 collective-permute-start
  63.8 1.3 collective-permute-start.1
  65.7 1.9 collective-permute-done.1
  67.5 8.8 %concatenate.38 = bf16[2,1182,384]{2,1,0:T(8,128)(2,1)S(1)} concatenate(bf16[2,15,384]{2,1,0:T(8,128)(2,1)S(1)} %collective-permute-done, bf16[2,1152,384]{2,1,0:T(8,128)(2,1)} %copy-done.6, bf16[2,15,384]{2,1,0:T(8,128)(2,1)S(1)} %collective-permute-done.1), dimensions={1} | concatenate | bytes 3631104 | tf_op jit(solution)/shard_map/concatenate | solution.py:18
  77.3 14.7 %multiply_reduce_fusion.34 = (f32[384]{0:T(512)S(1)}, f32[2,1152,384]{2,1,0:T(8,128)S(1)}) fusion(f32[2,1152]{1,0:T(2,128)S(1)} %compare_convert_fusion, f32[384]{0:T(512)S(1)} %copy-done.39, f32[2,1182,384]{2,1,0:T(8,128)S(1)} %convert_element_type.79, f32[384]{0:T(512)S(1)} %copy-done.40, f32[384]{0:T(512)S(1)} %copy-done.10, f32[384]{0:T(512)S(1)} %copy-done.11, ...), kind=kLoop, calls=%fused_computation.209 | loop fusion | flops 55737984 | bytes 113304576 | tf_op jit(solution)/shard_map/reduce_sum | solution.py:64
  92.1 14.1 %all-gather.1 = f32[8,1,384]{2,1,0:T(1,128)} all-gather(f32[1,1,384]{2,1,0:T(1,128)S(1)} %reshape.178), channel_id=2, replica_groups=mesh['ctx'=8,'chan'=4] {'ctx'}, dimensions={0}, use_global_device_ids=true | all-gather | bytes 13824 | tf_op jit(solution)/shard_map/all_gather | solution.py:64
  106.2 1.3 reduce_sum.390
  107.5 1.3 broadcast_divide_fusion
  110.5 15.5 %psum.49 = f32[384]{0:T(512)} all-reduce(f32[384]{0:T(512)} %multiply_reduce_fusion.33), channel_id=1, replica_groups=mesh['ctx'=8,'chan'=4] {'ctx'}, use_global_device_ids=true, to_apply=%region_6.0 | all-reduce | flops 384 | bytes 3072 | tf_op jit(solution)/shard_map/psum | solution.py:68
  125.9 1.9 fusion.110
  127.9 10.3 %fusion.108 = (f32[384]{0:T(512)}, f32[384]{0:T(512)}, bf16[2,1152,384]{2,1,0:T(8,128)(2,1)}, f32[2,1152,384]{2,1,0:T(8,128)}) fusion(f32[384]{0:T(512)} %get-tuple-element.106, f32[2,1152,384]{2,1,0:T(8,128)S(1)} %get-tuple-element.108, f32[384]{0:T(512)} %copy-done.28, f32[2,1152]{1,0:T(2,128)S(1)} %compare_convert_fusion, f32[384]{0:T(512)} %param.16, ...), kind=kOutput, calls=%fused_computation.260 | convolution fusion | flops 2734717952 | bytes 17123328 | tf_op jit(solution)/shard_map/dot_general | solution.py:91
  138.2 14.3 %all-reduce.1 = (f32[384]{0:T(512)}, f32[384]{0:T(512)}) all-reduce(f32[384]{0:T(512)} %get-tuple-element.62, f32[384]{0:T(512)} %get-tuple-element.61), channel_id=1, replica_groups=mesh['ctx'=8,'chan'=4] {'ctx'}, use_global_device_ids=true, to_apply=%region_11.0 | all-reduce | flops 768 | bytes 6144 | tf_op jit(solution)/shard_map/psum | solution.py:96
  152.5 40.0 %multiply_reduce_fusion.1 = (f32[384]{0:T(512)}, f32[384]{0:T(512)}, f32[384]{0:T(512)}, f32[384]{0:T(512)}, f32[384]{0:T(512)}, /*index=5*/f32[384]{0:T(512)}, ...) fusion(f32[2,1182,384]{2,1,0:T(8,128)} %copy-done, ...), kind=kLoop, calls=%fused_computation.169 | loop fusion | flops 38921472 | bytes 74362368 | tf_op jit(solution)/shard_map/reduce_sum | solution.py:107
  194.4 3.7 collective-permute-start.3
  198.0 7.0 %fusion.106 = bf16[1536,384]{0,1:T(8,128)(2,1)} fusion(bf16[2,1152,384]{2,1,0:T(8,128)(2,1)S(1)} %copy-done.64, bf16[2,1152,1536]{2,1,0:T(8,128)(2,1)} %param.19), kind=kOutput, calls=%fused_computation.216 | convolution fusion | flops 2718498816 | bytes 10027008 | tf_op jit(solution)/shard_map/dot_general | solution.py:23
  205.0 2.4 copy.47
  207.7 33.2 %multiply_bitcast_fusion.1 = (bf16[2,1152,1,384]{3,1,0,2:T(8,128)(2,1)S(1)}, f32[2,1152,384]{2,1,0:T(8,128)S(1)}) fusion(f32[2,1152,2,384]{3,1,2,0:T(8,128)} %copy-done.3, f32[2,1152]{1,0:T(2,128)S(1)} %compare_convert_fusion, f32[384]{0:T(512)} %get-tuple-element.94, f32[2,1152,384]{2,1,0:T(8,128)S(1)} %get-tuple-element.102, ...), kind=kLoop, calls=%fused_computation.201 | loop fusion | flops 85819392 | bytes 12535296 | tf_op jit(solution)/shard_map/stack | solution.py:119
  240.9 4.2 multiply_bitcast_fusion
  245.6 34.2 %copy.33 = bf16[2,1152,2,384]{3,2,1,0:T(2,128)(2,1)S(1)} copy(bf16[2,1152,2,384]{3,1,0,2:T(8,128)(2,1)S(1)} %maximum_convert_fusion) | data formatting | bytes 7077888 | tf_op jit(solution)/shard_map/convert_element_type | solution.py:120
  279.8 2.4 copy.51
  282.2 5.8 %copy.34 = bf16[768,2304]{1,0:T(8,128)(2,1)} copy(bf16[768,2304]{0,1:T(8,128)(2,1)} %bitcast.81) | data formatting | bytes 7077888 | tf_op jit(solution)/shard_map/dot_general | solution.py:23
  288.0 10.0 %convolution_convert_fusion.2 = bf16[1536,2,384]{2,0,1:T(8,128)(2,1)} fusion(bf16[2304,1536,1]{1,0,2:T(8,128)(2,1)} %bitcast.86, bf16[2,384,2304]{2,1,0:T(8,128)(2,1)} %bitcast.87), kind=kOutput, calls=%fused_computation.212 | convolution fusion | flops 5436997632 | bytes 12976128 | tf_op jit(solution)/shard_map/dot_general | solution.py:23
  298.1 8.5 %convolution_convert_fusion.1 = bf16[2304,1536]{1,0:T(8,128)(2,1)} fusion(bf16[2304,384]{1,0:T(8,128)(2,1)} %bitcast.95, bf16[1536,384]{1,0:T(8,128)(2,1)} %all-gather.7.cloned.1.call-done), kind=kOutput, calls=%fused_computation.32 | convolution fusion | flops 2721447936 | bytes 10027008 | tf_op jit(solution)/shard_map/dot_general | solution.py:23
  306.6 10.2 %copy.43 = bf16[2304,1536]{0,1:T(8,128)(2,1)} copy(bf16[2304,1536]{1,0:T(8,128)(2,1)} %convolution_convert_fusion.1) | data formatting | bytes 14155776
  317.1 10.3 %convolution_convert_fusion = bf16[2304,1536]{1,0:T(8,128)(2,1)} fusion(bf16[2304,768]{1,0:T(8,128)(2,1)} %bitcast.82, bf16[1536,768]{1,0:T(8,128)(2,1)} %bitcast.85), kind=kOutput, calls=%fused_computation.31 | convolution fusion | flops 5439356928 | bytes 12976128 | tf_op jit(solution)/shard_map/dot_general | solution.py:23
  327.4 9.9 %copy.45 = bf16[2304,1536]{0,1:T(8,128)(2,1)} copy(bf16[2304,1536]{1,0:T(8,128)(2,1)} %convolution_convert_fusion) | data formatting | bytes 14155776
  339.3 10.8 %bitcast_convert_fusion = f32[2304,1536]{1,0:T(8,128)} fusion(bf16[2,1152,1536]{2,1,0:T(8,128)(2,1)} %param.10), kind=kLoop, calls=%fused_computation.264 | loop fusion | flops 3538944 | bytes 21233664 | tf_op jit(solution)/shard_map/reshape | solution.py:79
  350.4 6.0 %multiply_reduce_fusion.2 = (f32[384]{0:T(512)S(1)}, f32[384]{0:T(512)S(1)}, f32[384]{0:T(512)S(1)}, f32[384]{0:T(512)S(1)}, f32[384]{0:T(512)S(1)}, /*index=5*/...) fusion(f32[2,1152,384]{2,1,0:T(8,128)S(1)} %get-tuple-element.1, ...), kind=kLoop, calls=%fused_computation.170 | loop fusion | flops 22998144 | bytes 49565184 | tf_op jit(solution)/shard_map/reduce_sum | solution.py:107
  359.5 2.1 copy.37
  361.6 50.4 %reduce-scatter.13.cloned.1.call-done = bf16[384,2304]{1,0:T(8,128)(2,1)} async-done(((bf16[1536,2304]{1,0:T(8,128)(2,1)}), bf16[384,2304]{1,0:T(8,128)(2,1)}) %reduce-scatter.13.cloned.1.call-update) | async-done | bytes 1769488
  412.0 2.8 copy.44
  414.8 3.6 add_convert_fusion.1
  418.4 73.2 %reduce-scatter.15.cloned.1.call-done = bf16[384,2304]{1,0:T(8,128)(2,1)} async-done(((bf16[1536,2304]{1,0:T(8,128)(2,1)}), bf16[384,2304]{1,0:T(8,128)(2,1)}) %reduce-scatter.15.cloned.1.call-update) | async-done | bytes 1769488
  491.5 2.8 copy.46
  494.3 3.2 fusion.11
  497.6 29.4 %all-reduce = (f32[31,384]{1,0:T(8,128)}, f32[2,384]{1,0:T(2,128)}) all-reduce(f32[31,384]{1,0:T(8,128)S(1)} %stack.157, f32[2,384]{1,0:T(2,128)S(1)} %pad_maximum_fusion.3), channel_id=1, replica_groups=mesh['ctx'=8,'chan'=4] {'ctx'}, use_global_device_ids=true, to_apply=%region_50.0 | all-reduce | flops 12672 | bytes 101376 | tf_op jit(solution)/shard_map/psum | solution.py:155
  527.0 15.4 %all-reduce.2 = (f32[2304]{0:T(1024)S(1)}, f32[2304]{0:T(1024)S(1)}) all-reduce(f32[2304]{0:T(1024)S(1)} %get-tuple-element.29, f32[2304]{0:T(1024)S(1)} %get-tuple-element.63), channel_id=1, replica_groups=mesh['ctx'=8,'chan'=4] {'chan'}, use_global_device_ids=true, to_apply=%region_16.0 | all-reduce | flops 4608 | bytes 36864 | tf_op jit(solution)/shard_map/psum | solution.py:142
  542.5 4.5 fusion.9
  (203 shorter events, 15.6 us)
Async XLA Ops:
  7.2 36.6 %all-gather.5.cloned.1.call-start = ((), (), s32[]{:S(2)}) async-start(), calls=%async_computation.4 | async-start | bytes 2654208 | tf_op jit(solution)/shard_map/all_gather | solution.py:48
  7.9 120.0 %all-gather.7.cloned.1.call-start = ((), (), s32[]{:S(2)}) async-start(), calls=%async_computation.5 | async-start | bytes 1327104 | tf_op jit(solution)/shard_map/all_gather | solution.py:75
  8.6 349.0 %reduce-scatter.17.cloned.1.call-start = ((), (), s32[]{:S(2)}) async-start(), calls=%async_computation.9 | async-start | bytes 1327104
  12.2 5.0 copy-start.2
  17.2 2.0 copy-start.63
  17.3 2.1 copy-start.41
  17.3 2.1 copy-start.42
  19.3 10.9 %copy-start.7 = (f32[2,1152]{1,0:T(2,128)}, f32[2,1152]{1,0:T(2,128)S(1)}, u32[]{:S(2)}) copy-start(f32[2,1152]{1,0:T(2,128)S(1)} %add_rsqrt_fusion) | copy-start | bytes 27652
  45.9 11.6 %copy-start.5 = (bf16[192,8,2,384]{3,1,2,0:T(8,128)(2,1)}, bf16[192,8,2,384]{3,1,2,0:T(8,128)(2,1)S(1)}, u32[]{:S(2)}) copy-start(bf16[192,8,2,384]{3,1,2,0:T(8,128)(2,1)S(1)} %copy.50) | copy-start | bytes 7077892
  57.5 2.9 copy-start.3
  60.4 1.2 copy-start.6
  61.7 4.0 collective-permute-start
  63.8 3.8 collective-permute-start.1
  76.5 0.7 copy-start.29
  76.5 0.7 copy-start.30
  76.6 0.7 copy-start.35
  76.6 0.7 copy-start.40
  76.9 15.1 %copy-start = (f32[2,1182,384]{2,1,0:T(8,128)}, f32[2,1182,384]{2,1,0:T(8,128)S(1)}, u32[]{:S(2)}) copy-start(f32[2,1182,384]{2,1,0:T(8,128)S(1)} %convert_element_type.79) | copy-start | bytes 10893316
  92.0 46.1 %copy-start.4 = (f32[2,1152,384]{2,1,0:T(8,128)}, f32[2,1152,384]{2,1,0:T(8,128)S(1)}, u32[]{:S(2)}) copy-start(f32[2,1152,384]{2,1,0:T(8,128)S(1)} %get-tuple-element.108) | copy-start | bytes 10616836
  152.5 45.6 %copy-start.64 = (bf16[2,1152,384]{2,1,0:T(8,128)(2,1)S(1)}, bf16[2,1152,384]{2,1,0:T(8,128)(2,1)}, u32[]{:S(2)}) copy-start(bf16[2,1152,384]{2,1,0:T(8,128)(2,1)} %get-tuple-element.111) | copy-start | bytes 5308420
  193.1 14.6 %collective-permute-start.2 = (f32[2,15,384]{2,1,0:T(8,128)}, f32[2,15,384]{2,1,0:T(8,128)}, u32[]{:S(2)}, u32[]{:S(2)}) collective-permute-start(f32[2,15,384]{2,1,0:T(8,128)} %get-tuple-element.112), channel_id=1, source_target_pairs={{4,0},{8,4},{12,8},{16,12},{20,16},{24,20},{28,24},{5,1},{9,5},{13... | collective-permute-start | bytes 138248 | tf_op jit(solution)/shard_map/ppermute | solution.py:17
  194.4 13.3 %collective-permute-start.3 = (f32[2,15,384]{2,1,0:T(8,128)}, f32[2,15,384]{2,1,0:T(8,128)}, u32[]{:S(2)}, u32[]{:S(2)}) collective-permute-start(f32[2,15,384]{2,1,0:T(8,128)} %get-tuple-element.113), channel_id=1, source_target_pairs={{0,4},{4,8},{8,12},{12,16},{16,20},{20,24},{24,28},{1,5},{5,9},{9,... | collective-permute-start | bytes 138248 | tf_op jit(solution)/shard_map/ppermute | solution.py:16
  207.5 152.1 %reduce-scatter.11.cloned.1.call-start = ((), (), s32[]{:S(2)}) async-start(), calls=%async_computation.6 | async-start | bytes 2654208 | tf_op jit(solution)/shard_map/reduce_scatter | solution.py:124
  298.1 113.9 %reduce-scatter.13.cloned.1.call-start = ((), (), s32[]{:S(2)}) async-start(), calls=%async_computation.7 | async-start | bytes 8847360
  316.8 174.7 %reduce-scatter.15.cloned.1.call-start = ((), (), s32[]{:S(2)}) async-start(), calls=%async_computation.8 | async-start | bytes 8847360
  337.3 0.7 copy-start.8
  339.3 10.8 %copy-start.62 = (f32[384]{0:T(512)S(1)}, f32[384]{0:T(512)}, u32[]{:S(2)}) copy-start(f32[384]{0:T(512)} %get-tuple-element.98) | copy-start | bytes 4612
  339.3 10.8 %copy-start.61 = (f32[384]{0:T(512)S(1)}, f32[384]{0:T(512)}, u32[]{:S(2)}) copy-start(f32[384]{0:T(512)} %get-tuple-element.99) | copy-start | bytes 4612
  339.3 10.8 %copy-start.1 = (f32[2,1182,384]{2,1,0:T(8,128)S(1)}, f32[2,1182,384]{2,1,0:T(8,128)}, u32[]{:S(2)}) copy-start(f32[2,1182,384]{2,1,0:T(8,128)} %copy-done) | copy-start | bytes 10893316
  350.2 6.3 %copy-start.60 = (f32[384]{0:T(512)S(1)}, f32[384]{0:T(512)}, u32[]{:S(2)}) copy-start(f32[384]{0:T(512)} %get-tuple-element.47) | copy-start | bytes 4612
  350.2 6.3 %copy-start.59 = (f32[384]{0:T(512)S(1)}, f32[384]{0:T(512)}, u32[]{:S(2)}) copy-start(f32[384]{0:T(512)} %get-tuple-element.46) | copy-start | bytes 4612
  350.2 6.4 %copy-start.58 = (f32[384]{0:T(512)S(1)}, f32[384]{0:T(512)}, u32[]{:S(2)}) copy-start(f32[384]{0:T(512)} %get-tuple-element.45) | copy-start | bytes 4612
  350.2 6.4 %copy-start.57 = (f32[384]{0:T(512)S(1)}, f32[384]{0:T(512)}, u32[]{:S(2)}) copy-start(f32[384]{0:T(512)} %get-tuple-element.44) | copy-start | bytes 4612
  350.2 6.4 %copy-start.56 = (f32[384]{0:T(512)S(1)}, f32[384]{0:T(512)}, u32[]{:S(2)}) copy-start(f32[384]{0:T(512)} %get-tuple-element.43) | copy-start | bytes 4612
  350.3 6.4 %copy-start.55 = (f32[384]{0:T(512)S(1)}, f32[384]{0:T(512)}, u32[]{:S(2)}) copy-start(f32[384]{0:T(512)} %get-tuple-element.42) | copy-start | bytes 4612
  350.3 6.4 %copy-start.54 = (f32[384]{0:T(512)S(1)}, f32[384]{0:T(512)}, u32[]{:S(2)}) copy-start(f32[384]{0:T(512)} %get-tuple-element.41) | copy-start | bytes 4612
  350.3 6.4 %copy-start.53 = (f32[384]{0:T(512)S(1)}, f32[384]{0:T(512)}, u32[]{:S(2)}) copy-start(f32[384]{0:T(512)} %get-tuple-element.40) | copy-start | bytes 4612
  350.3 6.4 %copy-start.52 = (f32[384]{0:T(512)S(1)}, f32[384]{0:T(512)}, u32[]{:S(2)}) copy-start(f32[384]{0:T(512)} %get-tuple-element.39) | copy-start | bytes 4612
  350.3 6.4 %copy-start.51 = (f32[384]{0:T(512)S(1)}, f32[384]{0:T(512)}, u32[]{:S(2)}) copy-start(f32[384]{0:T(512)} %get-tuple-element.38) | copy-start | bytes 4612
  350.3 6.4 %copy-start.50 = (f32[384]{0:T(512)S(1)}, f32[384]{0:T(512)}, u32[]{:S(2)}) copy-start(f32[384]{0:T(512)} %get-tuple-element.37) | copy-start | bytes 4612
  350.3 6.5 %copy-start.49 = (f32[384]{0:T(512)S(1)}, f32[384]{0:T(512)}, u32[]{:S(2)}) copy-start(f32[384]{0:T(512)} %get-tuple-element.36) | copy-start | bytes 4612
  350.3 6.5 %copy-start.48 = (f32[384]{0:T(512)S(1)}, f32[384]{0:T(512)}, u32[]{:S(2)}) copy-start(f32[384]{0:T(512)} %get-tuple-element.35) | copy-start | bytes 4612
  350.3 6.5 %copy-start.47 = (f32[384]{0:T(512)S(1)}, f32[384]{0:T(512)}, u32[]{:S(2)}) copy-start(f32[384]{0:T(512)} %get-tuple-element.34) | copy-start | bytes 4612
  350.3 6.5 %copy-start.46 = (f32[384]{0:T(512)S(1)}, f32[384]{0:T(512)}, u32[]{:S(2)}) copy-start(f32[384]{0:T(512)} %get-tuple-element.33) | copy-start | bytes 4612
  350.4 6.5 %copy-start.45 = (f32[384]{0:T(512)S(1)}, f32[384]{0:T(512)}, u32[]{:S(2)}) copy-start(f32[384]{0:T(512)} %get-tuple-element.32) | copy-start | bytes 4612
  350.4 6.5 %copy-start.44 = (f32[384]{0:T(512)S(1)}, f32[384]{0:T(512)}, u32[]{:S(2)}) copy-start(f32[384]{0:T(512)} %get-tuple-element.31) | copy-start | bytes 4612
  350.4 6.5 %copy-start.43 = (f32[384]{0:T(512)S(1)}, f32[384]{0:T(512)}, u32[]{:S(2)}) copy-start(f32[384]{0:T(512)} %get-tuple-element.30) | copy-start | bytes 4612
  494.3 48.2 %copy-start.9 = (f32[2304]{0:T(1024)S(1)}, f32[2304]{0:T(1024)}, u32[]{:S(2)}) copy-start(f32[2304]{0:T(1024)} %rsqrt.20) | copy-start | bytes 27652
  (27 other events, 18.1 us)
Sparse Core Ops, SparseCore 0:
  9.6 34.1 all-gather.4
  45.4 22.0 all-gather.6
  207.6 31.3 reduce-scatter.16
  298.2 35.4 reduce-scatter.10
  336.6 75.3 reduce-scatter.12
  414.9 76.5 reduce-scatter.14
